TPU v7x, 128 devices: a whole 4x4x4 slice. The times are simulated.
128 devices in a mesh: grp: 8 (over y, x_lo), bal: 16 (over x_hi, z, core).
Axes of the slice: x: 4 (x_hi: 2, x_lo: 2; x = x_hi * 2 + x_lo), y: 4, z: 4, core: 2. Of those that a mesh axis runs over, the one named last changes fastest.
Arguments:
- events: bfloat16 [8, 8192, 512], P('grp', 'bal'), may hold values from -6 to 6
- cotangent: bfloat16 [8, 8192, 512], P('grp', 'bal'), may hold values from -6 to 6
- lengths: int32 [8, 16], P('grp'), may hold values from 1 to 16, as said below
- gain_in: float32 [512], replicated, may hold values from 0.1 to 1.9
- w_proj: bfloat16 [512, 2048], replicated, may hold values from -0.25 to 0.25
- gain_attn: float32 [512], replicated, may hold values from 0.1 to 1.9
- w_out: bfloat16 [512, 512], replicated, may hold values from -0.25 to 0.25
Outputs:
- d_x: bfloat16 [8, 8192, 512], P('grp', 'bal')
- grad_proj: float32 [512, 2048], replicated
- grad_out: float32 [512, 512], replicated
- grad_gain_in: float32 [512], replicated
- grad_gain_attn: float32 [512], replicated
Inputs may be any that keep to these rules, and one draw needn't show every extreme that they name: A group's 16 lengths count blocks of 64 events and sum to 128; in every group one length equals 16.
All inputs are finite; a program needn't handle non-finite values.
Results may differ from a plain program's by a relative error of at most 0.013.
Values may be sent and summed in bfloat16 or wider, within the bound.
No kernel may reach another device: no remote copies, remote signals or barrier semaphores. Data moves between devices by JAX's collectives and lax.ppermute only.
A program may use at most 256 MiB of HBM per device.

v0:
```python
import math
import jax
import jax.numpy as jnp
from jax import lax
from jax.sharding import PartitionSpec as P

HEADS = 8
BLOCK = 64
LEN_BLK = 16
epsilon = 1e-06


def norm_rows(values):
    mean_value = jnp.mean(values, axis=-1, keepdims=True)
    centred = values - mean_value
    rstd = lax.rsqrt(jnp.mean(centred * centred, axis=-1, keepdims=True) + epsilon)
    return (centred * rstd, rstd)


def silu_slope(values):
    sigma = jax.nn.sigmoid(values)
    return sigma * (1.0 + values * (1.0 - sigma))


def norm_back(grad, normed, rstd):
    return rstd * (
        grad
        - jnp.mean(grad, axis=-1, keepdims=True)
        - normed * jnp.mean(grad * normed, axis=-1, keepdims=True)
    )


def contract_rows(left, right):
    return lax.dot_general(
        left, right, (((0,), (0,)), ((), ())), preferred_element_type=jnp.float32
    )


def contract_cols(left, right):
    return lax.dot_general(
        left, right, (((1,), (1,)), ((), ())), preferred_element_type=jnp.float32
    )


def project_rows(rows, gain_in, w_proj):
    normed, rstd_in = norm_rows(rows.astype(jnp.float32))
    scaled = (normed * gain_in).astype(jnp.bfloat16)
    hidden = jnp.dot(scaled, w_proj, preferred_element_type=jnp.float32)
    active = jax.nn.silu(hidden).astype(jnp.bfloat16)
    return (normed, rstd_in, scaled, hidden, active)


def output_rows(attn, upper, grads_out, gain_attn, w_out):
    normed, rstd = norm_rows(attn.astype(jnp.float32))
    upper_wide = upper.astype(jnp.float32)
    mixed = (normed * gain_attn * upper_wide).astype(jnp.bfloat16)
    d_mixed = contract_cols(grads_out, w_out)
    d_upper = d_mixed * normed * gain_attn
    d_attn = norm_back(d_mixed * gain_attn * upper_wide, normed, rstd).astype(jnp.bfloat16)
    out_term = contract_rows(mixed, grads_out)
    gain_term = jnp.sum(d_mixed * normed * upper_wide, axis=0)
    return (d_upper, d_attn, out_term, gain_term)


def input_rows(grads_out, d_act, hidden, normed, rstd_in, scaled, gain_in, w_proj):
    d_hidden = (d_act * silu_slope(hidden)).astype(jnp.bfloat16)
    proj_term = contract_rows(scaled, d_hidden)
    d_scaled = contract_cols(d_hidden, w_proj)
    d_rows = (
        grads_out.astype(jnp.float32) + norm_back(d_scaled * gain_in, normed, rstd_in)
    ).astype(jnp.bfloat16)
    gain_term = jnp.sum(d_scaled * normed, axis=0)
    return (d_rows, proj_term, gain_term)


def attend_forward(query, keys, values, allowed):
    head_width = query.shape[1] // HEADS
    scale = head_width ** (-0.5)
    outputs = []
    for head in range(HEADS):
        columns = slice(head * head_width, (head + 1) * head_width)
        scores = contract_cols(query[:, columns], keys[:, columns]) * scale
        weights = (jax.nn.silu(scores) * allowed).astype(jnp.bfloat16)
        outputs.append(jnp.dot(weights, values[:, columns], preferred_element_type=jnp.float32))
    return jnp.concatenate(outputs, axis=1).astype(jnp.bfloat16)


def attend_backward(query, keys, values, grad_attn, allowed):
    head_width = query.shape[1] // HEADS
    scale = head_width ** (-0.5)
    grads_query, grads_keys, grads_values = ([], [], [])
    for head in range(HEADS):
        columns = slice(head * head_width, (head + 1) * head_width)
        query_head = query[:, columns]
        key_head = keys[:, columns]
        grad_head = grad_attn[:, columns]
        scores = contract_cols(query_head, key_head) * scale
        weights = (jax.nn.silu(scores) * allowed).astype(jnp.bfloat16)
        grad_weights = contract_cols(grad_head, values[:, columns])
        grad_scores = (grad_weights * silu_slope(scores) * allowed).astype(jnp.bfloat16)
        grads_values.append(contract_rows(weights, grad_head).astype(jnp.bfloat16))
        grads_query.append(
            (jnp.dot(grad_scores, key_head, preferred_element_type=jnp.float32) * scale).astype(
                jnp.bfloat16
            )
        )
        grads_keys.append((contract_rows(grad_scores, query_head) * scale).astype(jnp.bfloat16))
    return (
        jnp.concatenate(grads_query, axis=1),
        jnp.concatenate(grads_keys, axis=1),
        jnp.concatenate(grads_values, axis=1),
    )


def lookup(table, positions):
    entries = jnp.arange(table.shape[0], dtype=jnp.int32)
    picked = jnp.where(entries[None, :] == positions[:, None], table[None, :], 0)
    return jnp.sum(picked, axis=1)


def regroup(table, rows):
    blocks = rows.reshape(table.shape[1], -1)
    moved = jnp.dot(table, blocks, preferred_element_type=jnp.float32)
    return moved.astype(jnp.bfloat16).reshape(-1, rows.shape[1])


def pack_histories(seq_lengths):

    def advance(state, length_now):
        device_rank, held_blocks = state
        fresh = held_blocks + length_now > LEN_BLK
        device_rank = device_rank + fresh.astype(jnp.int32)
        held_blocks = jnp.where(fresh, 0, held_blocks) + length_now
        return ((device_rank, held_blocks), device_rank)

    start_state = (jnp.int32(0), jnp.int32(0))
    final_state, ranks = lax.scan(advance, start_state, seq_lengths)
    return ranks


def held_tiles_map(tile_fn, live_tiles, inputs, tile_rows):
    count = inputs[0].shape[0] // tile_rows
    pieces = tuple((array.reshape((count, tile_rows) + array.shape[1:]) for array in inputs))

    def blank_fn(parts):
        return jax.tree.map(jnp.zeros_like, tile_fn(parts))

    def each_tile(item):
        position, parts = item
        return lax.cond(position < live_tiles, tile_fn, blank_fn, parts)

    return lax.map(each_tile, (jnp.arange(count, dtype=jnp.int32), pieces))


def flatten_tiles(array):
    return array.reshape((-1,) + array.shape[2:])


def whole_layer(rows, grads_out, allowed, live_tiles, tile_rows, gain_in, w_proj, gain_attn, w_out):
    width = rows.shape[1]
    first = held_tiles_map(
        lambda parts: project_rows(parts[0], gain_in, w_proj), live_tiles, (rows,), tile_rows
    )
    normed, rstd_in, scaled, hidden, active = jax.tree.map(flatten_tiles, first)
    upper = active[:, :width]
    values = active[:, width : 2 * width]
    query = active[:, 2 * width : 3 * width]
    keys = active[:, 3 * width :]
    attn = attend_forward(query, keys, values, allowed)
    second = held_tiles_map(
        lambda parts: output_rows(parts[0], parts[1], parts[2], gain_attn, w_out),
        live_tiles,
        (attn, upper, grads_out),
        tile_rows,
    )
    d_upper = flatten_tiles(second[0])
    d_attn = flatten_tiles(second[1])
    out_term = jnp.sum(second[2], axis=0)
    gain_attn_term = jnp.sum(second[3], axis=0)
    d_query, d_keys, d_values = attend_backward(query, keys, values, d_attn, allowed)
    d_act = jnp.concatenate(
        [
            d_upper,
            d_values.astype(jnp.float32),
            d_query.astype(jnp.float32),
            d_keys.astype(jnp.float32),
        ],
        axis=1,
    )
    third = held_tiles_map(
        lambda parts: input_rows(
            parts[0], parts[1], parts[2], parts[3], parts[4], parts[5], gain_in, w_proj
        ),
        live_tiles,
        (grads_out, d_act, hidden, normed, rstd_in, scaled),
        tile_rows,
    )
    d_rows = flatten_tiles(third[0])
    proj_term = jnp.sum(third[1], axis=0)
    gain_in_term = jnp.sum(third[2], axis=0)
    return (d_rows, (proj_term, out_term, gain_in_term, gain_attn_term))


def per_device(events, cotangent, lengths, gain_in, w_proj, gain_attn, w_out):
    peers = lax.axis_size("bal")
    own_index = lax.axis_index("bal")
    local_rows = events[0]
    local_grads = cotangent[0]
    local_blocks = local_rows.shape[0] // BLOCK
    slots = LEN_BLK // peers
    seq_lengths = lengths[0]
    targets = pack_histories(seq_lengths)
    ends = jnp.cumsum(seq_lengths)
    device_ids = jnp.arange(peers, dtype=jnp.int32)
    range_starts = jnp.sum(
        jnp.where(targets[None, :] < device_ids[:, None], seq_lengths[None, :], 0), axis=1
    )
    range_sizes = jnp.sum(
        jnp.where(targets[None, :] == device_ids[:, None], seq_lengths[None, :], 0), axis=1
    )
    flat_blocks = own_index + peers * jnp.arange(local_blocks, dtype=jnp.int32)
    owner_seq = jnp.sum((ends[None, :] <= flat_blocks[:, None]).astype(jnp.int32), axis=1)
    owner = lookup(targets, owner_seq)
    slot_index = (flat_blocks - lookup(range_starts, owner)) // peers
    slot_ids = jnp.arange(peers * slots, dtype=jnp.int32)
    send_table = (slot_ids[:, None] == (owner * slots + slot_index)[None, :]).astype(jnp.bfloat16)
    mine_start = lookup(range_starts, own_index[None])[0]
    mine_size = lookup(range_sizes, own_index[None])[0]
    block_order = jnp.arange(LEN_BLK, dtype=jnp.int32)
    from_slot = (mine_start + block_order) % peers * slots + block_order // peers
    take_table = (from_slot[:, None] == slot_ids[None, :]).astype(jnp.bfloat16)
    return_table = jnp.transpose(take_table)
    home_table = jnp.transpose(send_table)
    block_seq = jnp.sum(
        (ends[None, :] <= (mine_start + block_order)[:, None]).astype(jnp.int32), axis=1
    )
    block_seq = jnp.where(block_order < mine_size, block_seq, -1)
    row_seq = jnp.repeat(block_seq, BLOCK)
    positions = jnp.arange(LEN_BLK * BLOCK, dtype=jnp.int32)
    allowed = (
        (row_seq[:, None] == row_seq[None, :])
        & (row_seq[:, None] >= 0)
        & (positions[None, :] <= positions[:, None])
    ).astype(jnp.float32)
    tile_blocks = math.gcd(LEN_BLK, max(1, 256 // BLOCK))
    live_tiles = (mine_size + tile_blocks - 1) // tile_blocks
    got_rows, got_grads = (
        lax.all_to_all(
            regroup(send_table, local_rows), "bal", split_axis=0, concat_axis=0, tiled=True
        ),
        lax.all_to_all(
            regroup(send_table, local_grads), "bal", split_axis=0, concat_axis=0, tiled=True
        ),
    )
    held_rows = regroup(take_table, got_rows)
    held_grads = regroup(take_table, got_grads)
    d_held, terms = whole_layer(
        held_rows,
        held_grads,
        allowed,
        live_tiles,
        tile_blocks * BLOCK,
        gain_in,
        w_proj,
        gain_attn,
        w_out,
    )
    came_back = lax.all_to_all(
        regroup(return_table, d_held), "bal", split_axis=0, concat_axis=0, tiled=True
    )
    d_rows = regroup(home_table, came_back)
    sums = lax.psum((terms[0], terms[1], terms[2], terms[3]), ("grp", "bal"))
    divisor = float(lax.axis_size("grp") * peers)
    return (
        d_rows[None],
        sums[0] / divisor,
        sums[1] / divisor,
        sums[2] / divisor,
        sums[3] / divisor,
    )


def solution(mesh):
    placed = (P("grp", "bal", None), P("grp", "bal", None), P("grp", None), P(), P(), P(), P())
    return jax.shard_map(
        per_device,
        mesh=mesh,
        in_specs=placed,
        out_specs=(P("grp", "bal", None), P(), P(), P(), P()),
        check_vma=False,
    )
```

profile of v0, /device:TPU:1, one launch (start us, length us, event | category | flops | bytes accessed | tf_op | source)
XLA Modules:
  0.0 636.9 jit_solution(15162623421532527161)
XLA Ops:
  7.2 42.6 %while.66 = (s32[]{:T(128)}, s32[]{:T(128)}, s32[]{:T(128)}, s32[16]{0:T(128)S(1)}, s32[16]{0:T(128)}) while((s32[]{:T(128)}, s32[]{:T(128)}, s32[]{:T(128)}, s32[16]{0:T(128)S(1)}, s32[16]{0:T(128)}) %tuple.198), condition=%wide.region_3.4_spmd.clone, body=%wide.region_2.3_spmd.sunk.clone | while | flops 8 | bytes 148 | solution.py:137
  55.1 9.3 %all-to-all-start.1 = ((bf16[16,64,512]{2,1,0:T(8,128)(2,1)}), bf16[16,64,512]{2,1,0:T(8,128)(2,1)S(1)}, u32[]{:S(2)}, u32[]{:S(2)}) async-start(bf16[16,64,512]{2,1,0:T(8,128)(2,1)} %bitcast.70), calls=%async_computation.1 | async-start | bytes 2097152 | tf_op jit(solution)/shard_map/all_to_all | solution.py:248
  70.0 11.6 %all-to-all-done.1 = bf16[16,64,512]{2,1,0:T(8,128)(2,1)S(1)} async-done(((bf16[16,64,512]{2,1,0:T(8,128)(2,1)}), bf16[16,64,512]{2,1,0:T(8,128)(2,1)S(1)}, u32[]{:S(2)}, u32[]{:S(2)}) %all-to-all-start.1) | async-done | bytes 1048608 | tf_op jit(solution)/shard_map/all_to_all | solution.py:248
  81.6 5.0 all-to-all-start
  91.9 70.2 %while.67 = (s32[]{:T(128)}, f32[4,256,512]{2,1,0:T(8,128)}, f32[4,256,1]{1,2,0:T(1,128)}, bf16[4,256,512]{2,1,0:T(8,128)(2,1)}, f32[4,256,2048]{2,1,0:T(8,128)}...) while((s32[]{:T(128)}, f32[4,256,512]{2,1,0:T(8,128)}, ...), condition=%wide.region_16.17_spmd.clone, body=%wide.region_11.16_spmd.sunk.clone | while | flops 541589760 | bytes 17060060 | solution.py:152
  93.2 9.2 %conditional.9 = (f32[1,256,512]{2,1,0:T(8,128)S(1)}, f32[1,256,1]{1,2,0:T(1,128)}, bf16[1,256,512]{2,1,0:T(8,128)(2,1)S(1)}, f32[1,256,2048]{2,1,0:T(8,128)}, bf16[1,256,2048]{2,1,0:T(8,128)(2,1)S(1)}) conditional(s32[]{:T(128)} %convert_element_type.475, () %tuple.157, (bf16[4,256,512]{2,1,0:T(8,128)(2,1)}, s32[]{:T(128)}, f32[512]{0:T(512)S(1)}, ...), branch_computations={%region_12.12_spmd, %region_13.15_spmd} | conditional | flops 541589760 | bytes 9190964 | solution.py:150
  96.0 3.1 fusion.8
  102.4 3.2 constant_dynamic-update-slice_fusion.33
  110.8 9.2 %conditional.9 = (f32[1,256,512]{2,1,0:T(8,128)S(1)}, f32[1,256,1]{1,2,0:T(1,128)}, bf16[1,256,512]{2,1,0:T(8,128)(2,1)S(1)}, f32[1,256,2048]{2,1,0:T(8,128)}, bf16[1,256,2048]{2,1,0:T(8,128)(2,1)S(1)}) conditional(s32[]{:T(128)} %convert_element_type.475, () %tuple.157, (bf16[4,256,512]{2,1,0:T(8,128)(2,1)}, s32[]{:T(128)}, f32[512]{0:T(512)S(1)}, ...), branch_computations={%region_12.12_spmd, %region_13.15_spmd} | conditional | flops 541589760 | bytes 9190964 | solution.py:150
  113.6 3.1 fusion.8
  120.0 3.1 constant_dynamic-update-slice_fusion.33
  128.4 9.2 %conditional.9 = (f32[1,256,512]{2,1,0:T(8,128)S(1)}, f32[1,256,1]{1,2,0:T(1,128)}, bf16[1,256,512]{2,1,0:T(8,128)(2,1)S(1)}, f32[1,256,2048]{2,1,0:T(8,128)}, bf16[1,256,2048]{2,1,0:T(8,128)(2,1)S(1)}) conditional(s32[]{:T(128)} %convert_element_type.475, () %tuple.157, (bf16[4,256,512]{2,1,0:T(8,128)(2,1)}, s32[]{:T(128)}, f32[512]{0:T(512)S(1)}, ...), branch_computations={%region_12.12_spmd, %region_13.15_spmd} | conditional | flops 541589760 | bytes 9190964 | solution.py:150
  131.2 3.1 fusion.8
  137.6 3.2 constant_dynamic-update-slice_fusion.33
  145.9 9.2 %conditional.9 = (f32[1,256,512]{2,1,0:T(8,128)S(1)}, f32[1,256,1]{1,2,0:T(1,128)}, bf16[1,256,512]{2,1,0:T(8,128)(2,1)S(1)}, f32[1,256,2048]{2,1,0:T(8,128)}, bf16[1,256,2048]{2,1,0:T(8,128)(2,1)S(1)}) conditional(s32[]{:T(128)} %convert_element_type.475, () %tuple.157, (bf16[4,256,512]{2,1,0:T(8,128)(2,1)}, s32[]{:T(128)}, f32[512]{0:T(512)S(1)}, ...), branch_computations={%region_12.12_spmd, %region_13.15_spmd} | conditional | flops 541589760 | bytes 9190964 | solution.py:150
  148.8 3.1 fusion.8
  155.2 3.1 constant_dynamic-update-slice_fusion.33
  162.2 3.7 fusion.113
  165.9 3.7 fusion.120
  169.6 3.7 fusion.127
  173.3 3.9 fusion.134
  177.2 3.7 fusion.141
  180.9 3.8 fusion.148
  186.4 19.1 %select_convert_fusion.8 = (bf16[1024,1024]{1,0:T(8,128)(2,1)S(1)}, bf16[1024,1024]{1,0:T(8,128)(2,1)}, bf16[1024,1024]{1,0:T(8,128)(2,1)}, bf16[1024,1024]{1,0:...) fusion(pred[1024]{0:T(1024)(128)(4,1)S(1)} %broadcast_compare_f, ...), kind=kOutput, calls=%fused_computation.122 | convolution fusion | flops 197132288 | bytes 50865152 | tf_op jit(solution)/shard_map/dot_general | solution.py:40
  237.3 35.1 %while.68 = (s32[]{:T(128)}, f32[4,256,512]{2,1,0:T(8,128)}, bf16[4,256,512]{2,1,0:T(8,128)(2,1)}, f32[4,512,512]{2,1,0:T(8,128)}, f32[4,512]{1,0:T(4,128)S(1)},...) while((s32[]{:T(128)}, f32[4,256,512]{2,1,0:T(8,128)}, ...), condition=%wide.region_25.26_spmd.clone, body=%wide.region_17.25_spmd.sunk.clone | while | flops 273415936 | bytes 9736943 | solution.py:152
  238.5 4.9 conditional.10
  247.3 4.9 conditional.10
  256.1 4.9 conditional.10
  264.8 4.9 conditional.10
  282.7 5.2 select_convert_fusion.1
  288.0 4.9 select_convert_fusion.2
  292.9 4.8 select_convert_fusion.3
  297.7 4.9 select_convert_fusion.4
  302.6 4.8 select_convert_fusion.5
  307.4 4.9 select_convert_fusion.6
  312.3 4.8 select_convert_fusion.7
  317.2 4.9 select_convert_fusion
  329.9 2.4 fusion.76
  338.4 2.4 fusion.74
  347.5 2.5 fusion.72
  372.0 5.6 pad_maximum_fusion
  377.8 67.9 %while.69 = (s32[]{:T(128)}, bf16[4,256,512]{2,1,0:T(8,128)(2,1)S(1)}, f32[4,512,2048]{2,1,0:T(8,128)}, f32[4,512]{1,0:T(4,128)S(1)}, s32[4]{0:T(128)S(1)}, /*in...) while((s32[]{:T(128)}, ...), condition=%wide.region_32.33_spmd.clone, body=%wide.region_26.32_spmd.sunk.clone | while | flops 1085013504 | bytes 26500880 | solution.py:152
  379.3 10.9 %conditional.11 = (bf16[1,256,512]{2,1,0:T(8,128)(2,1)S(1)}, f32[1,512,2048]{2,1,0:T(8,128)}, f32[1,512]{1,0:T(1,128)S(1)}) conditional(s32[]{:T(128)} %convert_element_type.477, () %tuple.167, (bf16[4,256,512]{2,1,0:T(8,128)(2,1)}, s32[]{:T(128)}, f32[4,256,1]{1,2,0:T(1,128)}, f32[4,256,2048]{2,1,0:T(8,128)}, f32[4,256,2048]{2,1,0:T(8,128)}, ...), branch_computations={%region_27.27_spmd, %region_28.31_spmd} | conditional | flops 1085013504 | bytes 17583136 | solution.py:150
  379.3 3.4 fusion.62
  384.7 5.5 convolution_bitcast_fusion.1
  390.2 4.6 constant_dynamic-update-slice_fusion.39
  396.1 10.9 %conditional.11 = (bf16[1,256,512]{2,1,0:T(8,128)(2,1)S(1)}, f32[1,512,2048]{2,1,0:T(8,128)}, f32[1,512]{1,0:T(1,128)S(1)}) conditional(s32[]{:T(128)} %convert_element_type.477, () %tuple.167, (bf16[4,256,512]{2,1,0:T(8,128)(2,1)}, s32[]{:T(128)}, f32[4,256,1]{1,2,0:T(1,128)}, f32[4,256,2048]{2,1,0:T(8,128)}, f32[4,256,2048]{2,1,0:T(8,128)}, ...), branch_computations={%region_27.27_spmd, %region_28.31_spmd} | conditional | flops 1085013504 | bytes 17583136 | solution.py:150
  396.2 3.4 fusion.62
  401.6 5.5 convolution_bitcast_fusion.1
  407.1 4.7 constant_dynamic-update-slice_fusion.39
  413.1 11.0 %conditional.11 = (bf16[1,256,512]{2,1,0:T(8,128)(2,1)S(1)}, f32[1,512,2048]{2,1,0:T(8,128)}, f32[1,512]{1,0:T(1,128)S(1)}) conditional(s32[]{:T(128)} %convert_element_type.477, () %tuple.167, (bf16[4,256,512]{2,1,0:T(8,128)(2,1)}, s32[]{:T(128)}, f32[4,256,1]{1,2,0:T(1,128)}, f32[4,256,2048]{2,1,0:T(8,128)}, f32[4,256,2048]{2,1,0:T(8,128)}, ...), branch_computations={%region_27.27_spmd, %region_28.31_spmd} | conditional | flops 1085013504 | bytes 17583136 | solution.py:150
  413.1 3.4 fusion.62
  418.5 5.5 convolution_bitcast_fusion.1
  424.0 4.7 constant_dynamic-update-slice_fusion.39
  430.0 11.0 %conditional.11 = (bf16[1,256,512]{2,1,0:T(8,128)(2,1)S(1)}, f32[1,512,2048]{2,1,0:T(8,128)}, f32[1,512]{1,0:T(1,128)S(1)}) conditional(s32[]{:T(128)} %convert_element_type.477, () %tuple.167, (bf16[4,256,512]{2,1,0:T(8,128)(2,1)}, s32[]{:T(128)}, f32[4,256,1]{1,2,0:T(1,128)}, f32[4,256,2048]{2,1,0:T(8,128)}, f32[4,256,2048]{2,1,0:T(8,128)}, ...), branch_computations={%region_27.27_spmd, %region_28.31_spmd} | conditional | flops 1085013504 | bytes 17583136 | solution.py:150
  430.0 3.4 fusion.62
  435.5 5.5 convolution_bitcast_fusion.1
  441.0 4.6 constant_dynamic-update-slice_fusion.39
  445.7 10.1 %reduce_sum.224 = f32[512,2048]{1,0:T(8,128)} reduce(f32[4,512,2048]{2,1,0:T(8,128)} %get-tuple-element.445, f32[]{:T(128)} %constant.270.clone.1), dimensions={0}, to_apply=%region_33.34 | reduce | flops 3145728 | bytes 20971524 | tf_op jit(solution)/shard_map/reduce_sum | solution.py:199
  455.8 3.8 reduce_sum.225
  462.0 5.8 all-to-all-start.2
  467.8 73.7 %all-reduce = (f32[512]{0:T(512)S(1)}, f32[512]{0:T(512)S(1)}) all-reduce(f32[512]{0:T(512)S(1)} %reduce_sum.226, f32[512]{0:T(512)S(1)} %reduce_sum.227), channel_id=1, replica_groups=mesh['grp'=8,'bal'=16] {'grp','bal'}, use_global_device_ids=true, to_apply=%region_38.39 | all-reduce | flops 1024 | bytes 8192 | tf_op jit(solution)/shard_map/psum | solution.py:272
  544.6 79.3 %all-reduce.4.cloned.1.call-done = (f32[512,2048]{1,0:T(8,128)}, f32[512,512]{1,0:T(8,128)}) async-done(((f32[512,2048]{1,0:T(8,128)}, f32[512,512]{1,0:T(8,128)}), (f32[512,2048]{1,0:T(8,128)}, f32[512,512]{1,0:T(8,128)})) %all-reduce.4.cloned.1.call-update) | async-done | bytes 5242896 | tf_op jit(solution)/shard_map/psum | solution.py:272
  623.9 4.9 broadcast_multiply_fusion.6
  (372 shorter events, 214.9 us)
Async XLA Ops:
  7.2 60.8 %copy-start.36 = (bf16[1,512,512]{2,1,0:T(8,128)(2,1)S(1)}, bf16[1,512,512]{2,1,0:T(8,128)(2,1)}, u32[]{:S(2)}) copy-start(bf16[1,512,512]{2,1,0:T(8,128)(2,1)} %param.22) | copy-start | bytes 1572868
  52.0 16.6 %copy-start.40 = (s32[8]{0:T(128)}, s32[8]{0:T(128)S(1)}, u32[]{:S(2)}) copy-start(s32[8]{0:T(128)S(1)} %fusion.169) | copy-start | bytes 100
  55.1 26.5 %all-to-all-start.1 = ((bf16[16,64,512]{2,1,0:T(8,128)(2,1)}), bf16[16,64,512]{2,1,0:T(8,128)(2,1)S(1)}, u32[]{:S(2)}, u32[]{:S(2)}) async-start(bf16[16,64,512]{2,1,0:T(8,128)(2,1)} %bitcast.70), calls=%async_computation.1 | async-start | bytes 2097152 | tf_op jit(solution)/shard_map/all_to_all | solution.py:248
  67.0 163.3 %copy-start.42 = (s32[16]{0:T(128)}, s32[16]{0:T(128)S(1)}, u32[]{:S(2)}) copy-start(s32[16]{0:T(128)S(1)} %get-tuple-element.578) | copy-start | bytes 196
  81.6 147.0 %all-to-all-start = ((bf16[16,64,512]{2,1,0:T(8,128)(2,1)}), bf16[16,64,512]{2,1,0:T(8,128)(2,1)}, u32[]{:S(2)}, u32[]{:S(2)}) async-start(bf16[16,64,512]{2,1,0:T(8,128)(2,1)} %bitcast.66), calls=%async_computation | async-start | bytes 2097152 | tf_op jit(solution)/shard_map/all_to_all | solution.py:251
  86.6 537.4 %all-reduce.4.cloned.1.call-start = ((), (), s32[]{:S(2)}) async-start(), calls=%async_computation.3 | async-start | bytes 10485760 | tf_op jit(solution)/shard_map/psum | solution.py:272
  87.2 4.8 copy-start
  87.2 4.8 copy-start.30
  186.4 19.1 %copy-start.15 = (f32[1024,1024]{1,0:T(8,128)}, f32[1024,1024]{1,0:T(8,128)S(1)}, u32[]{:S(2)}) copy-start(f32[1024,1024]{1,0:T(8,128)S(1)} %fusion.155) | copy-start | bytes 12582916
  205.5 7.7 %copy-start.8 = (bf16[1024,1024]{1,0:T(8,128)(2,1)}, bf16[1024,1024]{1,0:T(8,128)(2,1)S(1)}, u32[]{:S(2)}) copy-start(bf16[1024,1024]{1,0:T(8,128)(2,1)S(1)} %get-tuple-element.573) | copy-start | bytes 6291460
  205.5 7.7 %copy-start.10 = (bf16[1024,1024]{1,0:T(8,128)(2,1)}, bf16[1024,1024]{1,0:T(8,128)(2,1)S(1)}, u32[]{:S(2)}) copy-start(bf16[1024,1024]{1,0:T(8,128)(2,1)S(1)} %get-tuple-element.574) | copy-start | bytes 6291460
  205.5 7.7 %copy-start.6 = (bf16[1024,1024]{1,0:T(8,128)(2,1)}, bf16[1024,1024]{1,0:T(8,128)(2,1)S(1)}, u32[]{:S(2)}) copy-start(bf16[1024,1024]{1,0:T(8,128)(2,1)S(1)} %get-tuple-element.572) | copy-start | bytes 6291460
  205.5 9.4 %copy-start.12 = (bf16[1024,1024]{1,0:T(8,128)(2,1)}, bf16[1024,1024]{1,0:T(8,128)(2,1)S(1)}, u32[]{:S(2)}) copy-start(bf16[1024,1024]{1,0:T(8,128)(2,1)S(1)} %get-tuple-element.575) | copy-start | bytes 6291460
  205.5 9.4 %copy-start.13 = (bf16[1024,1024]{1,0:T(8,128)(2,1)}, bf16[1024,1024]{1,0:T(8,128)(2,1)S(1)}, u32[]{:S(2)}) copy-start(bf16[1024,1024]{1,0:T(8,128)(2,1)S(1)} %get-tuple-element.569) | copy-start | bytes 6291460
  205.5 20.4 %copy-start.2 = (bf16[1024,1024]{1,0:T(8,128)(2,1)}, bf16[1024,1024]{1,0:T(8,128)(2,1)S(1)}, u32[]{:S(2)}) copy-start(bf16[1024,1024]{1,0:T(8,128)(2,1)S(1)} %get-tuple-element.576) | copy-start | bytes 6291460
  227.7 4.5 copy-start.23
  227.7 4.5 copy-start.24
  230.8 6.4 %copy-start.37 = (f32[512]{0:T(512)S(1)}, f32[512]{0:T(512)}, u32[]{:S(2)}) copy-start(f32[512]{0:T(512)} %param.26) | copy-start | bytes 6148
  272.4 5.3 copy-start.38
  272.4 2.4 copy-start.14
  272.4 4.6 copy-start.11
  274.7 2.9 copy-start.9
  277.0 1.6 copy-start.7
  277.7 1.8 copy-start.5
  278.6 1.7 copy-start.4
  279.4 1.7 copy-start.3
  280.4 2.3 copy-start.22
  282.7 5.2 copy-start.21
  288.0 4.9 copy-start.20
  292.9 4.8 copy-start.19
  297.7 4.9 copy-start.18
  302.6 4.8 copy-start.17
  307.4 4.9 copy-start.16
  312.3 4.8 copy-start.44
  359.1 4.9 copy-start.32
  359.1 5.1 copy-start.33
  359.1 5.2 copy-start.34
  359.1 5.4 copy-start.35
  366.7 2.2 copy-start.26
  366.7 2.4 copy-start.27
  366.8 2.6 copy-start.28
  366.8 2.8 copy-start.29
  372.0 5.8 copy-start.1
  372.0 5.8 copy-start.31
  459.6 0.6 copy-start.43
  459.6 8.2 %copy-start.39 = (f32[4,512]{1,0:T(4,128)S(1)}, f32[4,512]{1,0:T(4,128)}, u32[]{:S(2)}) copy-start(f32[4,512]{1,0:T(4,128)} %copy-done.38) | copy-start | bytes 24580
  460.2 83.1 %copy-start.41 = (s32[8]{0:T(128)S(1)}, s32[8]{0:T(128)}, u32[]{:S(2)}) copy-start(s32[8]{0:T(128)} %copy-done.40) | copy-start | bytes 100
  462.0 80.6 %all-to-all-start.2 = ((bf16[16,64,512]{2,1,0:T(8,128)(2,1)}), bf16[16,64,512]{2,1,0:T(8,128)(2,1)S(1)}, u32[]{:S(2)}, u32[]{:S(2)}) async-start(bf16[16,64,512]{2,1,0:T(8,128)(2,1)} %bitcast.74), calls=%async_computation.2 | async-start | bytes 2097152 | tf_op jit(solution)/shard_map/all_to_all | solution.py:268
  623.9 4.9 copy-start.25
Sparse Core Ops, SparseCore 0:
  459.7 164.1 all-reduce.3
where the time goes:
time: 644 us; the launch traced here: 637 us
  matrix products  205 us (32%)
  local copies, waits for them, and re-layouts  132 us (20%)
  waiting for transfers between devices  90.9 us (14%)
  blocking collectives  73.7 us (11%)
  other arithmetic  70.4 us (11%)
  loops' own time  29.7 us (5%)
  starting transfers between devices  20.1 us (3%)
  between operations  16 us (2%)
    dot_general x24, matrix products, contract_cols(): lax.dot_general(left, right, (((1,), (1,)), ((), ())), preferred_element_...  103 us
    psum x1, waiting for transfers between devices, per_device(): sums = lax.psum((terms[0], terms[1], terms[2], terms[3]), ('grp', 'bal'))  79.3 us
    psum x1, blocking collectives, per_device(): sums = lax.psum((terms[0], terms[1], terms[2], terms[3]), ('grp', 'bal'))  73.7 us
    dynamic_update_slice x48, local copies, waits for them, and re-layouts, held_tiles_map(): return lax.map(each_tile, (jnp.arange(count, dtype=jnp.int32), pieces))  57.7 us
    dot_general x24, matrix products, contract_rows(): lax.dot_general(left, right, (((0,), (0,)), ((), ())), preferred_element_...  51.2 us
    another operation x1, loops' own time, pack_histories(): final_state, ranks = lax.scan(advance, start_state, seq_lengths)  20.9 us
    dynamic_slice x16, local copies, waits for them, and re-layouts, pack_histories(): final_state, ranks = lax.scan(advance, start_state, seq_lengths)  19.9 us
    dot_general x8, matrix products, attend_backward(): jnp.dot(grad_scores, key_head, preferred_element_type=jnp.float32) * scale  19.2 us
  transfers between devices with their start and end apart: 4, of which 2 were waited for; matrix products, arithmetic and copies ran while one was open for 23% of the time, Pallas kernels for 0%

commit v1 on v0

--- a/solution.py
+++ b/solution.py
@@ -269,7 +269,7 @@
         regroup(return_table, d_held), "bal", split_axis=0, concat_axis=0, tiled=True
     )
     d_rows = regroup(home_table, came_back)
-    sums = lax.psum((terms[0], terms[1], terms[2], terms[3]), ("grp", "bal"))
+    sums = lax.psum(lax.psum((terms[0], terms[1], terms[2], terms[3]), "bal"), "grp")
     divisor = float(lax.axis_size("grp") * peers)
     return (
         d_rows[None],

time: 644 us -> 869 us (1.35)
  waiting for transfers between devices: 90.9 us -> 317 us
    psum x1 -> x2, waiting for transfers between devices: 79.3 us -> 306 us  [the longest x1 153 us: per_device(): lax.psum((terms[0], terms[1], terms[2], terms[3]), 'bal')]
    psum x1 -> x2, blocking collectives: 73.7 us -> 70.1 us  [the longest x1 52.3 us: per_device(): lax.psum((terms[0], terms[1], terms[2], terms[3]), 'bal')]
  transfers between devices with their start and end apart: 4 -> 5, of which waited for: 2 -> 3; matrix products, arithmetic and copies ran while one was open for 23% -> 17% of each run, Pallas kernels for 0% -> 0%
where the time goes in v1:
time: 869 us; the launch traced here: 862 us
  waiting for transfers between devices  317 us (36%)
  matrix products  205 us (24%)
  local copies, waits for them, and re-layouts  132 us (15%)
  other arithmetic  70.4 us (8%)
  blocking collectives  70.1 us (8%)
  loops' own time  29.7 us (3%)
  starting transfers between devices  22 us (3%)
  between operations  16.1 us (2%)
    psum x1, waiting for transfers between devices, per_device(): lax.psum((terms[0], terms[1], terms[2], terms[3]), 'bal')  153 us
    psum x1, waiting for transfers between devices, per_device(): lax.psum(lax.psum((terms[0], terms[1], terms[2], terms[3]), 'bal'), 'grp')  153 us
    dot_general x24, matrix products, contract_cols(): lax.dot_general(left, right, (((1,), (1,)), ((), ())), preferred_element_...  103 us
    dynamic_update_slice x48, local copies, waits for them, and re-layouts, held_tiles_map(): return lax.map(each_tile, (jnp.arange(count, dtype=jnp.int32), pieces))  57.7 us
    psum x1, blocking collectives, per_device(): lax.psum((terms[0], terms[1], terms[2], terms[3]), 'bal')  52.3 us
    dot_general x24, matrix products, contract_rows(): lax.dot_general(left, right, (((0,), (0,)), ((), ())), preferred_element_...  51.2 us
    another operation x1, loops' own time, pack_histories(): final_state, ranks = lax.scan(advance, start_state, seq_lengths)  20.9 us
    dynamic_slice x16, local copies, waits for them, and re-layouts, pack_histories(): final_state, ranks = lax.scan(advance, start_state, seq_lengths)  19.9 us
  transfers between devices with their start and end apart: 5, of which 3 were waited for; matrix products, arithmetic and copies ran while one was open for 17% of the time, Pallas kernels for 0%

profile of v1, /device:TPU:1, one launch (start us, length us, event | category | flops | bytes accessed | tf_op | source)
XLA Modules:
  0.0 861.8 jit_solution(5402769518485513113)
XLA Ops:
  7.2 42.6 %while.66 = (s32[]{:T(128)}, s32[]{:T(128)}, s32[]{:T(128)}, s32[16]{0:T(128)S(1)}, s32[16]{0:T(128)}) while((s32[]{:T(128)}, s32[]{:T(128)}, s32[]{:T(128)}, s32[16]{0:T(128)S(1)}, s32[16]{0:T(128)}) %tuple.201), condition=%wide.region_3.4_spmd.clone, body=%wide.region_2.3_spmd.sunk.clone | while | flops 8 | bytes 148 | solution.py:137
  55.1 9.3 %all-to-all-start.1 = ((bf16[16,64,512]{2,1,0:T(8,128)(2,1)}), bf16[16,64,512]{2,1,0:T(8,128)(2,1)S(1)}, u32[]{:S(2)}, u32[]{:S(2)}) async-start(bf16[16,64,512]{2,1,0:T(8,128)(2,1)} %bitcast.70), calls=%async_computation.1 | async-start | bytes 2097152 | tf_op jit(solution)/shard_map/all_to_all | solution.py:248
  70.0 11.6 %all-to-all-done.1 = bf16[16,64,512]{2,1,0:T(8,128)(2,1)S(1)} async-done(((bf16[16,64,512]{2,1,0:T(8,128)(2,1)}), bf16[16,64,512]{2,1,0:T(8,128)(2,1)S(1)}, u32[]{:S(2)}, u32[]{:S(2)}) %all-to-all-start.1) | async-done | bytes 1048608 | tf_op jit(solution)/shard_map/all_to_all | solution.py:248
  81.6 5.0 all-to-all-start
  91.9 70.2 %while.67 = (s32[]{:T(128)}, f32[4,256,512]{2,1,0:T(8,128)}, f32[4,256,1]{1,2,0:T(1,128)}, bf16[4,256,512]{2,1,0:T(8,128)(2,1)}, f32[4,256,2048]{2,1,0:T(8,128)}...) while((s32[]{:T(128)}, f32[4,256,512]{2,1,0:T(8,128)}, ...), condition=%wide.region_16.17_spmd.clone, body=%wide.region_11.16_spmd.sunk.clone | while | flops 541589760 | bytes 17060060 | solution.py:152
  93.2 9.2 %conditional.9 = (f32[1,256,512]{2,1,0:T(8,128)S(1)}, f32[1,256,1]{1,2,0:T(1,128)}, bf16[1,256,512]{2,1,0:T(8,128)(2,1)S(1)}, f32[1,256,2048]{2,1,0:T(8,128)}, bf16[1,256,2048]{2,1,0:T(8,128)(2,1)S(1)}) conditional(s32[]{:T(128)} %convert_element_type.475, () %tuple.157, (bf16[4,256,512]{2,1,0:T(8,128)(2,1)}, s32[]{:T(128)}, f32[512]{0:T(512)S(1)}, ...), branch_computations={%region_12.12_spmd, %region_13.15_spmd} | conditional | flops 541589760 | bytes 9190964 | solution.py:150
  96.0 3.1 fusion.8
  102.4 3.2 constant_dynamic-update-slice_fusion.33
  110.8 9.2 %conditional.9 = (f32[1,256,512]{2,1,0:T(8,128)S(1)}, f32[1,256,1]{1,2,0:T(1,128)}, bf16[1,256,512]{2,1,0:T(8,128)(2,1)S(1)}, f32[1,256,2048]{2,1,0:T(8,128)}, bf16[1,256,2048]{2,1,0:T(8,128)(2,1)S(1)}) conditional(s32[]{:T(128)} %convert_element_type.475, () %tuple.157, (bf16[4,256,512]{2,1,0:T(8,128)(2,1)}, s32[]{:T(128)}, f32[512]{0:T(512)S(1)}, ...), branch_computations={%region_12.12_spmd, %region_13.15_spmd} | conditional | flops 541589760 | bytes 9190964 | solution.py:150
  113.6 3.1 fusion.8
  120.0 3.1 constant_dynamic-update-slice_fusion.33
  128.4 9.2 %conditional.9 = (f32[1,256,512]{2,1,0:T(8,128)S(1)}, f32[1,256,1]{1,2,0:T(1,128)}, bf16[1,256,512]{2,1,0:T(8,128)(2,1)S(1)}, f32[1,256,2048]{2,1,0:T(8,128)}, bf16[1,256,2048]{2,1,0:T(8,128)(2,1)S(1)}) conditional(s32[]{:T(128)} %convert_element_type.475, () %tuple.157, (bf16[4,256,512]{2,1,0:T(8,128)(2,1)}, s32[]{:T(128)}, f32[512]{0:T(512)S(1)}, ...), branch_computations={%region_12.12_spmd, %region_13.15_spmd} | conditional | flops 541589760 | bytes 9190964 | solution.py:150
  131.2 3.1 fusion.8
  137.6 3.2 constant_dynamic-update-slice_fusion.33
  145.9 9.2 %conditional.9 = (f32[1,256,512]{2,1,0:T(8,128)S(1)}, f32[1,256,1]{1,2,0:T(1,128)}, bf16[1,256,512]{2,1,0:T(8,128)(2,1)S(1)}, f32[1,256,2048]{2,1,0:T(8,128)}, bf16[1,256,2048]{2,1,0:T(8,128)(2,1)S(1)}) conditional(s32[]{:T(128)} %convert_element_type.475, () %tuple.157, (bf16[4,256,512]{2,1,0:T(8,128)(2,1)}, s32[]{:T(128)}, f32[512]{0:T(512)S(1)}, ...), branch_computations={%region_12.12_spmd, %region_13.15_spmd} | conditional | flops 541589760 | bytes 9190964 | solution.py:150
  148.8 3.1 fusion.8
  155.2 3.1 constant_dynamic-update-slice_fusion.33
  162.2 3.7 fusion.113
  165.9 3.7 fusion.120
  169.6 3.7 fusion.127
  173.3 3.9 fusion.134
  177.2 3.7 fusion.141
  180.9 3.8 fusion.148
  186.4 19.1 %select_convert_fusion.8 = (bf16[1024,1024]{1,0:T(8,128)(2,1)S(1)}, bf16[1024,1024]{1,0:T(8,128)(2,1)}, bf16[1024,1024]{1,0:T(8,128)(2,1)}, bf16[1024,1024]{1,0:...) fusion(pred[1024]{0:T(1024)(128)(4,1)S(1)} %broadcast_compare_f, ...), kind=kOutput, calls=%fused_computation.122 | convolution fusion | flops 197132288 | bytes 50865152 | tf_op jit(solution)/shard_map/dot_general | solution.py:40
  237.3 35.1 %while.68 = (s32[]{:T(128)}, f32[4,256,512]{2,1,0:T(8,128)}, bf16[4,256,512]{2,1,0:T(8,128)(2,1)}, f32[4,512,512]{2,1,0:T(8,128)}, f32[4,512]{1,0:T(4,128)S(1)},...) while((s32[]{:T(128)}, f32[4,256,512]{2,1,0:T(8,128)}, ...), condition=%wide.region_25.26_spmd.clone, body=%wide.region_17.25_spmd.sunk.clone | while | flops 273415936 | bytes 9736943 | solution.py:152
  238.5 4.9 conditional.10
  247.3 4.9 conditional.10
  256.1 4.9 conditional.10
  264.8 4.9 conditional.10
  282.7 5.2 select_convert_fusion.1
  288.0 4.9 select_convert_fusion.2
  292.9 4.8 select_convert_fusion.3
  297.7 4.9 select_convert_fusion.4
  302.6 4.8 select_convert_fusion.5
  307.4 4.9 select_convert_fusion.6
  312.3 4.8 select_convert_fusion.7
  317.2 4.9 select_convert_fusion
  347.5 2.5 fusion.72
  372.0 5.6 pad_maximum_fusion
  377.8 67.9 %while.69 = (s32[]{:T(128)}, bf16[4,256,512]{2,1,0:T(8,128)(2,1)S(1)}, f32[4,512,2048]{2,1,0:T(8,128)}, f32[4,512]{1,0:T(4,128)S(1)}, s32[4]{0:T(128)S(1)}, /*in...) while((s32[]{:T(128)}, ...), condition=%wide.region_32.33_spmd.clone, body=%wide.region_26.32_spmd.sunk.clone | while | flops 1085013504 | bytes 26500880 | solution.py:152
  379.3 10.9 %conditional.11 = (bf16[1,256,512]{2,1,0:T(8,128)(2,1)S(1)}, f32[1,512,2048]{2,1,0:T(8,128)}, f32[1,512]{1,0:T(1,128)S(1)}) conditional(s32[]{:T(128)} %convert_element_type.477, () %tuple.167, (bf16[4,256,512]{2,1,0:T(8,128)(2,1)}, s32[]{:T(128)}, f32[4,256,1]{1,2,0:T(1,128)}, f32[4,256,2048]{2,1,0:T(8,128)}, f32[4,256,2048]{2,1,0:T(8,128)}, ...), branch_computations={%region_27.27_spmd, %region_28.31_spmd} | conditional | flops 1085013504 | bytes 17583136 | solution.py:150
  379.3 3.4 fusion.62
  384.7 5.5 convolution_bitcast_fusion.1
  390.2 4.6 constant_dynamic-update-slice_fusion.39
  396.1 10.9 %conditional.11 = (bf16[1,256,512]{2,1,0:T(8,128)(2,1)S(1)}, f32[1,512,2048]{2,1,0:T(8,128)}, f32[1,512]{1,0:T(1,128)S(1)}) conditional(s32[]{:T(128)} %convert_element_type.477, () %tuple.167, (bf16[4,256,512]{2,1,0:T(8,128)(2,1)}, s32[]{:T(128)}, f32[4,256,1]{1,2,0:T(1,128)}, f32[4,256,2048]{2,1,0:T(8,128)}, f32[4,256,2048]{2,1,0:T(8,128)}, ...), branch_computations={%region_27.27_spmd, %region_28.31_spmd} | conditional | flops 1085013504 | bytes 17583136 | solution.py:150
  396.2 3.4 fusion.62
  401.6 5.5 convolution_bitcast_fusion.1
  407.1 4.7 constant_dynamic-update-slice_fusion.39
  413.1 11.0 %conditional.11 = (bf16[1,256,512]{2,1,0:T(8,128)(2,1)S(1)}, f32[1,512,2048]{2,1,0:T(8,128)}, f32[1,512]{1,0:T(1,128)S(1)}) conditional(s32[]{:T(128)} %convert_element_type.477, () %tuple.167, (bf16[4,256,512]{2,1,0:T(8,128)(2,1)}, s32[]{:T(128)}, f32[4,256,1]{1,2,0:T(1,128)}, f32[4,256,2048]{2,1,0:T(8,128)}, f32[4,256,2048]{2,1,0:T(8,128)}, ...), branch_computations={%region_27.27_spmd, %region_28.31_spmd} | conditional | flops 1085013504 | bytes 17583136 | solution.py:150
  413.1 3.4 fusion.62
  418.5 5.5 convolution_bitcast_fusion.1
  424.0 4.7 constant_dynamic-update-slice_fusion.39
  430.0 11.0 %conditional.11 = (bf16[1,256,512]{2,1,0:T(8,128)(2,1)S(1)}, f32[1,512,2048]{2,1,0:T(8,128)}, f32[1,512]{1,0:T(1,128)S(1)}) conditional(s32[]{:T(128)} %convert_element_type.477, () %tuple.167, (bf16[4,256,512]{2,1,0:T(8,128)(2,1)}, s32[]{:T(128)}, f32[4,256,1]{1,2,0:T(1,128)}, f32[4,256,2048]{2,1,0:T(8,128)}, f32[4,256,2048]{2,1,0:T(8,128)}, ...), branch_computations={%region_27.27_spmd, %region_28.31_spmd} | conditional | flops 1085013504 | bytes 17583136 | solution.py:150
  430.0 3.4 fusion.62
  435.5 5.5 convolution_bitcast_fusion.1
  441.0 4.6 constant_dynamic-update-slice_fusion.39
  445.7 10.1 %reduce_sum.224 = f32[512,2048]{1,0:T(8,128)} reduce(f32[4,512,2048]{2,1,0:T(8,128)} %get-tuple-element.445, f32[]{:T(128)} %constant.270.clone.1), dimensions={0}, to_apply=%region_33.34 | reduce | flops 3145728 | bytes 20971524 | tf_op jit(solution)/shard_map/reduce_sum | solution.py:199
  455.8 3.7 reduce_sum.225
  459.6 153.0 %all-reduce.7.cloned.1.call-done = (f32[512,2048]{1,0:T(8,128)}, f32[512,512]{1,0:T(8,128)}) async-done(((f32[512,2048]{1,0:T(8,128)}, f32[512,512]{1,0:T(8,128)}), (f32[512,2048]{1,0:T(8,128)}, f32[512,512]{1,0:T(8,128)})) %all-reduce.7.cloned.1.call-update) | async-done | bytes 5242896 | tf_op jit(solution)/shard_map/psum | solution.py:272
  615.1 7.6 all-to-all-start.2
  622.8 52.3 %all-reduce = (f32[512]{0:T(512)S(1)}, f32[512]{0:T(512)S(1)}) all-reduce(f32[512]{0:T(512)S(1)} %reduce_sum.226, f32[512]{0:T(512)S(1)} %reduce_sum.227), channel_id=1, replica_groups=mesh['grp'=8,'bal'=16] {'bal'}, use_global_device_ids=true, to_apply=%region_40.41 | all-reduce | flops 1024 | bytes 8192 | tf_op jit(solution)/shard_map/psum | solution.py:272
  675.1 17.8 %all-reduce.2 = (f32[512]{0:T(512)S(1)}, f32[512]{0:T(512)S(1)}) all-reduce(f32[512]{0:T(512)S(1)} %get-tuple-element.555, f32[512]{0:T(512)S(1)} %get-tuple-element.556), channel_id=1, replica_groups=mesh['grp'=8,'bal'=16] {'grp'}, use_global_device_ids=true, to_apply=%region_41.42 | all-reduce | flops 1024 | bytes 8192 | tf_op jit(solution)/shard_map/psum | solution.py:272
  696.0 152.8 %all-reduce.9.cloned.1.call-done = (f32[512,2048]{1,0:T(8,128)}, f32[512,512]{1,0:T(8,128)}) async-done(((f32[512,2048]{1,0:T(8,128)}, f32[512,512]{1,0:T(8,128)}), (f32[512,2048]{1,0:T(8,128)}, f32[512,512]{1,0:T(8,128)})) %all-reduce.9.cloned.1.call-update) | async-done | bytes 5242896 | tf_op jit(solution)/shard_map/psum | solution.py:272
  848.8 4.9 broadcast_multiply_fusion.6
  (376 shorter events, 219.9 us)
Async XLA Ops:
  7.2 60.8 %copy-start.36 = (bf16[1,512,512]{2,1,0:T(8,128)(2,1)S(1)}, bf16[1,512,512]{2,1,0:T(8,128)(2,1)}, u32[]{:S(2)}) copy-start(bf16[1,512,512]{2,1,0:T(8,128)(2,1)} %param.22) | copy-start | bytes 1572868
  52.0 16.6 %copy-start.40 = (s32[8]{0:T(128)}, s32[8]{0:T(128)S(1)}, u32[]{:S(2)}) copy-start(s32[8]{0:T(128)S(1)} %fusion.169) | copy-start | bytes 100
  55.1 26.5 %all-to-all-start.1 = ((bf16[16,64,512]{2,1,0:T(8,128)(2,1)}), bf16[16,64,512]{2,1,0:T(8,128)(2,1)S(1)}, u32[]{:S(2)}, u32[]{:S(2)}) async-start(bf16[16,64,512]{2,1,0:T(8,128)(2,1)} %bitcast.70), calls=%async_computation.1 | async-start | bytes 2097152 | tf_op jit(solution)/shard_map/all_to_all | solution.py:248
  67.0 163.3 %copy-start.42 = (s32[16]{0:T(128)}, s32[16]{0:T(128)S(1)}, u32[]{:S(2)}) copy-start(s32[16]{0:T(128)S(1)} %get-tuple-element.582) | copy-start | bytes 196
  81.6 147.0 %all-to-all-start = ((bf16[16,64,512]{2,1,0:T(8,128)(2,1)}), bf16[16,64,512]{2,1,0:T(8,128)(2,1)}, u32[]{:S(2)}, u32[]{:S(2)}) async-start(bf16[16,64,512]{2,1,0:T(8,128)(2,1)} %bitcast.66), calls=%async_computation | async-start | bytes 2097152 | tf_op jit(solution)/shard_map/all_to_all | solution.py:251
  86.6 526.1 %all-reduce.7.cloned.1.call-start = ((), (), s32[]{:S(2)}) async-start(), calls=%async_computation.3 | async-start | bytes 10485760 | tf_op jit(solution)/shard_map/psum | solution.py:272
  87.2 4.8 copy-start
  87.2 4.8 copy-start.30
  186.4 19.1 %copy-start.15 = (f32[1024,1024]{1,0:T(8,128)}, f32[1024,1024]{1,0:T(8,128)S(1)}, u32[]{:S(2)}) copy-start(f32[1024,1024]{1,0:T(8,128)S(1)} %fusion.155) | copy-start | bytes 12582916
  205.5 7.7 copy-start.8
  205.5 7.7 copy-start.10
  205.5 7.7 copy-start.6
  205.5 9.4 %copy-start.12 = (bf16[1024,1024]{1,0:T(8,128)(2,1)}, bf16[1024,1024]{1,0:T(8,128)(2,1)S(1)}, u32[]{:S(2)}) copy-start(bf16[1024,1024]{1,0:T(8,128)(2,1)S(1)} %get-tuple-element.579) | copy-start | bytes 6291460
  205.5 9.4 %copy-start.13 = (bf16[1024,1024]{1,0:T(8,128)(2,1)}, bf16[1024,1024]{1,0:T(8,128)(2,1)S(1)}, u32[]{:S(2)}) copy-start(bf16[1024,1024]{1,0:T(8,128)(2,1)S(1)} %get-tuple-element.573) | copy-start | bytes 6291460
  205.5 20.4 %copy-start.2 = (bf16[1024,1024]{1,0:T(8,128)(2,1)}, bf16[1024,1024]{1,0:T(8,128)(2,1)S(1)}, u32[]{:S(2)}) copy-start(bf16[1024,1024]{1,0:T(8,128)(2,1)S(1)} %get-tuple-element.580) | copy-start | bytes 6291460
  227.7 4.5 copy-start.23
  227.7 4.5 copy-start.24
  230.8 6.4 copy-start.37
  272.4 5.3 copy-start.38
  272.4 2.4 copy-start.14
  272.4 4.6 copy-start.11
  274.7 2.9 copy-start.9
  277.0 1.6 copy-start.7
  277.7 1.8 copy-start.5
  278.6 1.7 copy-start.4
  279.4 1.7 copy-start.3
  280.4 2.3 copy-start.22
  282.7 5.2 copy-start.21
  288.0 4.9 copy-start.20
  292.9 4.8 copy-start.19
  297.7 4.9 copy-start.18
  302.6 4.8 copy-start.17
  307.4 4.9 copy-start.16
  312.3 4.8 copy-start.44
  359.1 4.9 copy-start.32
  359.1 5.1 copy-start.33
  359.1 5.2 copy-start.34
  359.1 5.4 copy-start.35
  366.7 2.2 copy-start.26
  366.7 2.4 copy-start.27
  366.8 2.6 copy-start.28
  366.8 2.8 copy-start.29
  372.0 5.8 copy-start.1
  372.0 5.8 copy-start.31
  459.6 153.7 %copy-start.43 = (s32[16]{0:T(128)S(1)}, s32[16]{0:T(128)}, u32[]{:S(2)}) copy-start(s32[16]{0:T(128)} %copy-done.42) | copy-start | bytes 196
  459.6 389.2 %all-reduce.9.cloned.1.call-start = ((), (), s32[]{:S(2)}) async-start(), calls=%async_computation.4 | async-start | bytes 10485760 | tf_op jit(solution)/shard_map/psum | solution.py:272
  612.7 10.1 %copy-start.39 = (f32[4,512]{1,0:T(4,128)S(1)}, f32[4,512]{1,0:T(4,128)}, u32[]{:S(2)}) copy-start(f32[4,512]{1,0:T(4,128)} %copy-done.38) | copy-start | bytes 24580
  613.2 81.4 %copy-start.41 = (s32[8]{0:T(128)S(1)}, s32[8]{0:T(128)}, u32[]{:S(2)}) copy-start(s32[8]{0:T(128)} %copy-done.40) | copy-start | bytes 100
  615.1 78.9 %all-to-all-start.2 = ((bf16[16,64,512]{2,1,0:T(8,128)(2,1)}), bf16[16,64,512]{2,1,0:T(8,128)(2,1)S(1)}, u32[]{:S(2)}, u32[]{:S(2)}) async-start(bf16[16,64,512]{2,1,0:T(8,128)(2,1)} %bitcast.74), calls=%async_computation.2 | async-start | bytes 2097152 | tf_op jit(solution)/shard_map/all_to_all | solution.py:268
  848.8 4.9 copy-start.25
Sparse Core Ops, SparseCore 0:
  459.7 152.9 all-reduce.6
  615.2 233.5 all-reduce.8
